TPU v7x, 32 devices: a whole 2x2x4 slice. The times are simulated.
32 devices in a mesh: row: 4 (over z), col: 8 (over y, x, core).
Axes of the slice: x: 2, y: 2, z: 4, core: 2. Of those that a mesh axis runs over, the one named last changes fastest.
Arguments:
- gaussian_sketch: bfloat16 [16384, 256], P(('col', 'row')), may hold values from -6 to 6
- block_values: bfloat16 [8192, 128, 128], P(('row', 'col')), may hold values from -6 to 6
- block_rows: int32 [8192], P(('row', 'col')), may hold values from 0 to 127, as said below
- block_columns: int32 [8192], P(('row', 'col')), may hold values from 0 to 127, as said below
Outputs:
- range_basis: float32 [16384, 256], P(('row', 'col'))
- upper_factor: float32 [256, 256], replicated
Inputs may be any that keep to these rules, and one draw needn't show every extreme that they name: `block_rows`: entry k * 256 + m, k = i * 8 + j, names a block row in [i * 32, (i + 1) * 32); no (row, column) pair is named twice. `block_columns`: entry k * 256 + m, k = i * 8 + j, names a block column in [j * 16, (j + 1) * 16).
All inputs are finite; a program needn't handle non-finite values.
Results may differ from a plain program's by a relative error of at most 0.0003.
Values may be sent and summed in bfloat16 or wider, within the bound.
No kernel may reach another device: no remote copies, remote signals or barrier semaphores. Data moves between devices by JAX's collectives and lax.ppermute only.
A program may use at most 128 MiB of HBM per device.

v0:
```python
import math
import jax
import jax.numpy as jnp
from jax import lax
from jax.sharding import PartitionSpec as P

PANEL = 128


def upper_parts(gram):
    lower_factor = jnp.linalg.cholesky(gram)
    identity = jnp.eye(gram.shape[0], dtype=gram.dtype)
    inverse = lax.linalg.triangular_solve(lower_factor, identity, left_side=True, lower=True)
    return (lower_factor.T, inverse.T)


def tile_product(sketch_blocks, block_values, local_rows, local_cols, tile_rows):
    group_size = math.gcd(block_values.shape[0], 64)
    col_width = sketch_blocks.shape[2]

    def advance(counter, summed):
        offset = (counter * group_size).astype(jnp.int32)
        values = lax.dynamic_slice_in_dim(block_values, offset, group_size, 0)
        row_ids = lax.dynamic_slice_in_dim(local_rows, offset, group_size, 0)
        col_ids = lax.dynamic_slice_in_dim(local_cols, offset, group_size, 0)
        picked = jnp.take(sketch_blocks, col_ids, axis=0)
        product = jnp.einsum("gab,gbs->gas", values, picked, preferred_element_type=jnp.float32)
        return summed.at[row_ids].add(product)

    initial = jnp.zeros((tile_rows, block_values.shape[1], col_width), jnp.float32)
    summed = lax.fori_loop(0, block_values.shape[0] // group_size, advance, initial)
    return summed.reshape(tile_rows * block_values.shape[1], col_width)


def on_device(gaussian_sketch, block_values, block_rows, block_columns):
    high = lax.Precision.HIGHEST
    size_row = lax.axis_size("row")
    size_col = lax.axis_size("col")
    shard_rows = gaussian_sketch.shape[0]
    block_size = block_values.shape[1]
    grid_rows = shard_rows * size_col // block_size
    grid_cols = shard_rows * size_row // block_size
    local_rows = block_rows - lax.axis_index("row") * grid_rows
    local_cols = block_columns - lax.axis_index("col") * grid_cols
    gathered = lax.all_gather(gaussian_sketch, "row", axis=0, tiled=True)
    sketch_blocks = gathered.reshape(grid_cols, block_size, gathered.shape[1])
    partial_value = tile_product(sketch_blocks, block_values, local_rows, local_cols, grid_rows)
    sketched = lax.psum_scatter(partial_value, "col", scatter_dimension=0, tiled=True)
    first_part = sketched[:, :PANEL]
    second_part = sketched[:, PANEL:]
    order_total = shard_rows * size_row * size_col
    gram_one = (
        lax.psum(jnp.dot(first_part.T, first_part, precision=high), ("row", "col")) / order_total
    )
    upper_one, inverse_one = upper_parts(gram_one)
    basis_one = jnp.dot(first_part, inverse_one, precision=high)
    coupling = (
        lax.psum(jnp.dot(basis_one.T, second_part, precision=high), ("row", "col")) / order_total
    )
    remainder = second_part - jnp.dot(basis_one, coupling, precision=high)
    gram_two = (
        lax.psum(jnp.dot(remainder.T, remainder, precision=high), ("row", "col")) / order_total
    )
    upper_two, inverse_two = upper_parts(gram_two)
    basis_two = jnp.dot(remainder, inverse_two, precision=high)
    range_basis = jnp.concatenate([basis_one, basis_two], axis=1)
    top_rows = jnp.concatenate([upper_one, coupling], axis=1)
    bottom_rows = jnp.concatenate([jnp.zeros_like(upper_two), upper_two], axis=1)
    upper_factor = jnp.concatenate([top_rows, bottom_rows], axis=0)
    return (range_basis, upper_factor)


def solution(mesh):
    return jax.shard_map(
        on_device,
        mesh=mesh,
        in_specs=(
            P(("col", "row"), None),
            P(("row", "col"), None, None),
            P(("row", "col")),
            P(("row", "col")),
        ),
        out_specs=(P(("row", "col"), None), P()),
        check_vma=False,
    )
```

profile of v0, /device:TPU:1, one launch (start us, length us, event | category | flops | bytes accessed | tf_op | source)
XLA Modules:
  0.0 643.8 jit_solution(3256187784970648376)
XLA Ops:
  7.2 0.7 all-gather.2.cloned.1.call-update
  8.0 0.7 broadcast_subtract_fusion
  8.7 30.8 %all-gather.2.cloned.1.call-done = bf16[2048,256]{1,0:T(8,128)(2,1)} async-done(((bf16[512,256]{1,0:T(8,128)(2,1)}), bf16[2048,256]{1,0:T(8,128)(2,1)}) %all-gather.2.cloned.1.call-update) | async-done | bytes 1048592 | tf_op jit(solution)/shard_map/all_gather | solution.py:45
  39.5 2.5 broadcast_in_dim.36
  41.9 118.3 %while.13 = (s32[]{:T(128)}, f32[32,128,256]{2,1,0:T(8,128)}, s32[256]{0:T(256)S(1)}, bf16[256,128,128]{2,1,0:T(8,128)(2,1)}, s32[256]{0:T(256)S(1)}, /*index=5*...) while((s32[]{:T(128)}, f32[32,128,256]{2,1,0:T(8,128)}, s32[256]{0:T(256)S(1)}, ...), condition=%wide.region_2.3_spmd, body=%wide.region_0.2_spmd.sunk | while | flops 541066816 | bytes 48240672 | solution.py:31
  41.9 0.1 compare_and_fusion.2
  42.0 2.8 gather_fusion
  44.8 7.4 %fusion.38 = f32[64,128,256]{2,1,0:T(8,128)} fusion(bf16[64,128,256]{2,1,0:T(8,128)(2,1)} %gather_fusion, pred[64]{0:T(512)(128)(4,1)S(1)} %get-tuple-element.176, bf16[256,128,128]{2,1,0:T(8,128)(2,1)} %get-tuple-element.200, s32[]{:T(128)S(6)} %select_n.59), kind=kOutput, calls=%fused_computation.2.clone.1 | convolution fusion | flops 538968064 | bytes 14680132 | tf_op jit(solution)/shard_map/while/body/eval_jaxpr/gab,gbs->gas/dot_general | solution.py:27
  52.3 19.2 %scatter_fusion = f32[32,128,256]{2,1,0:T(8,128)} fusion(f32[32,128,256]{2,1,0:T(8,128)} %get-tuple-element.188, s32[64]{0:T(128)S(1)} %compare_select_fusion.4, f32[64,128,256]{2,1,0:T(8,128)} %fusion.38), kind=kCustom, calls=%fused_computation.1.clone.1 | custom fusion | flops 2097152 | bytes 25166080 | tf_op jit(solution)/shard_map/while/body/eval_jaxpr/scatter-add | solution.py:28
  71.5 2.8 gather_fusion
  74.3 7.4 %fusion.38 = f32[64,128,256]{2,1,0:T(8,128)} fusion(bf16[64,128,256]{2,1,0:T(8,128)(2,1)} %gather_fusion, pred[64]{0:T(512)(128)(4,1)S(1)} %get-tuple-element.176, bf16[256,128,128]{2,1,0:T(8,128)(2,1)} %get-tuple-element.200, s32[]{:T(128)S(6)} %select_n.59), kind=kOutput, calls=%fused_computation.2.clone.1 | convolution fusion | flops 538968064 | bytes 14680132 | tf_op jit(solution)/shard_map/while/body/eval_jaxpr/gab,gbs->gas/dot_general | solution.py:27
  81.7 19.1 %scatter_fusion = f32[32,128,256]{2,1,0:T(8,128)} fusion(f32[32,128,256]{2,1,0:T(8,128)} %get-tuple-element.188, s32[64]{0:T(128)S(1)} %compare_select_fusion.4, f32[64,128,256]{2,1,0:T(8,128)} %fusion.38), kind=kCustom, calls=%fused_computation.1.clone.1 | custom fusion | flops 2097152 | bytes 25166080 | tf_op jit(solution)/shard_map/while/body/eval_jaxpr/scatter-add | solution.py:28
  101.0 2.8 gather_fusion
  103.7 7.4 %fusion.38 = f32[64,128,256]{2,1,0:T(8,128)} fusion(bf16[64,128,256]{2,1,0:T(8,128)(2,1)} %gather_fusion, pred[64]{0:T(512)(128)(4,1)S(1)} %get-tuple-element.176, bf16[256,128,128]{2,1,0:T(8,128)(2,1)} %get-tuple-element.200, s32[]{:T(128)S(6)} %select_n.59), kind=kOutput, calls=%fused_computation.2.clone.1 | convolution fusion | flops 538968064 | bytes 14680132 | tf_op jit(solution)/shard_map/while/body/eval_jaxpr/gab,gbs->gas/dot_general | solution.py:27
  111.2 19.6 %scatter_fusion = f32[32,128,256]{2,1,0:T(8,128)} fusion(f32[32,128,256]{2,1,0:T(8,128)} %get-tuple-element.188, s32[64]{0:T(128)S(1)} %compare_select_fusion.4, f32[64,128,256]{2,1,0:T(8,128)} %fusion.38), kind=kCustom, calls=%fused_computation.1.clone.1 | custom fusion | flops 2097152 | bytes 25166080 | tf_op jit(solution)/shard_map/while/body/eval_jaxpr/scatter-add | solution.py:28
  130.9 2.8 gather_fusion
  133.6 7.4 %fusion.38 = f32[64,128,256]{2,1,0:T(8,128)} fusion(bf16[64,128,256]{2,1,0:T(8,128)(2,1)} %gather_fusion, pred[64]{0:T(512)(128)(4,1)S(1)} %get-tuple-element.176, bf16[256,128,128]{2,1,0:T(8,128)(2,1)} %get-tuple-element.200, s32[]{:T(128)S(6)} %select_n.59), kind=kOutput, calls=%fused_computation.2.clone.1 | convolution fusion | flops 538968064 | bytes 14680132 | tf_op jit(solution)/shard_map/while/body/eval_jaxpr/gab,gbs->gas/dot_general | solution.py:27
  141.1 19.2 %scatter_fusion = f32[32,128,256]{2,1,0:T(8,128)} fusion(f32[32,128,256]{2,1,0:T(8,128)} %get-tuple-element.188, s32[64]{0:T(128)S(1)} %compare_select_fusion.4, f32[64,128,256]{2,1,0:T(8,128)} %fusion.38), kind=kCustom, calls=%fused_computation.1.clone.1 | custom fusion | flops 2097152 | bytes 25166080 | tf_op jit(solution)/shard_map/while/body/eval_jaxpr/scatter-add | solution.py:28
  160.3 50.9 %reduce-scatter.2.cloned.1.call-done = f32[512,256]{1,0:T(8,128)} async-done(((f32[4096,256]{1,0:T(8,128)}), f32[512,256]{1,0:T(8,128)}) %reduce-scatter.2.cloned.1.call-update) | async-done | bytes 524304 | tf_op jit(solution)/shard_map/reduce_scatter | solution.py:48
  211.2 2.2 fusion.11
  213.6 124.1 %all-reduce.5.cloned.1.call-done = f32[128,128]{0,1:T(8,128)} async-done(((f32[128,128]{0,1:T(8,128)}), f32[128,128]{0,1:T(8,128)}) %all-reduce.5.cloned.1.call-update) | async-done | bytes 65552 | tf_op jit(solution)/shard_map/psum | solution.py:53
  337.7 0.8 broadcast_multiply_fusion.2
  338.5 0.1 copy.7
  338.6 0.9 fusion.20
  339.5 11.7 %cholesky.44 = f32[128,128]{1,0:T(8,128)S(1)} custom-call(f32[128,128]{1,0:T(8,128)S(1)} %fusion.20), custom_call_target="Cholesky" | custom-call | tf_op jit(solution)/shard_map/jit(cholesky)/cholesky | solution.py:11
  351.2 0.6 compare_reduce_fusion.1
  351.8 0.7 fusion.22
  352.5 9.8 %custom-call.6 = f32[1,128,128]{1,2,0:T(8,128)S(1)} custom-call(f32[1,128,128]{2,1,0:T(8,128)S(1)} %get-tuple-element.131), custom_call_target="InvertDiagBlocksLowerTriangular" | custom-call | tf_op jit(solution)/shard_map/triangular_solve/custom-call.0 | solution.py:13
  362.3 0.3 fusion.15
  362.6 1.3 fusion.9
  364.0 2.2 fusion.7
  366.2 0.2 all-reduce.9.cloned.1.call-start
  366.4 118.3 %all-reduce.7.cloned.1.call-done = f32[128,128]{0,1:T(8,128)} async-done(((f32[128,128]{0,1:T(8,128)}), f32[128,128]{0,1:T(8,128)}) %all-reduce.7.cloned.1.call-update) | async-done | bytes 65552 | tf_op jit(solution)/shard_map/psum | solution.py:58
  484.7 1.6 convolution_subtract_fusion
  486.3 1.2 fusion.24
  487.5 0.8 broadcast_multiply_fusion.1
  488.3 121.6 %all-reduce.9.cloned.1.call-done = f32[128,128]{0,1:T(8,128)} async-done(((f32[128,128]{0,1:T(8,128)}), f32[128,128]{0,1:T(8,128)}) %all-reduce.9.cloned.1.call-update) | async-done | bytes 65552 | tf_op jit(solution)/shard_map/psum | solution.py:62
  610.0 0.8 broadcast_multiply_fusion
  610.8 0.1 copy.10
  610.9 0.9 fusion.18
  611.8 11.7 %cholesky.55 = f32[128,128]{1,0:T(8,128)S(1)} custom-call(f32[128,128]{1,0:T(8,128)S(1)} %fusion.18), custom_call_target="Cholesky" | custom-call | tf_op jit(solution)/shard_map/jit(cholesky)/cholesky | solution.py:11
  623.5 0.6 compare_reduce_fusion
  624.2 0.7 fusion.23
  624.8 0.8 copy.12
  625.7 9.8 %custom-call.7 = f32[1,128,128]{1,2,0:T(8,128)S(1)} custom-call(f32[1,128,128]{2,1,0:T(8,128)S(1)} %get-tuple-element.133), custom_call_target="InvertDiagBlocksLowerTriangular" | custom-call | tf_op jit(solution)/shard_map/triangular_solve/custom-call.0 | solution.py:13
  635.5 0.3 fusion.13
  635.8 0.4 fusion.25
  636.2 1.0 copy.11
  (25 shorter events, 0.9 us)
Async XLA Ops:
  7.2 32.3 %all-gather.2.cloned.1.call-start = ((), (), s32[]{:S(2)}) async-start(), calls=%async_computation.1 | async-start | bytes 1310720 | tf_op jit(solution)/shard_map/all_gather | solution.py:45
  7.9 203.3 %reduce-scatter.2.cloned.1.call-start = ((), (), s32[]{:S(2)}) async-start(), calls=%async_computation.2 | async-start | bytes 4718592 | tf_op jit(solution)/shard_map/reduce_scatter | solution.py:48
  39.5 2.5 copy-start
  160.3 177.4 %all-reduce.5.cloned.1.call-start = ((), (), s32[]{:S(2)}) async-start(), calls=%async_computation.3 | async-start | bytes 131072 | tf_op jit(solution)/shard_map/psum | solution.py:53
  213.5 271.2 %all-reduce.7.cloned.1.call-start = ((), (), s32[]{:S(2)}) async-start(), calls=%async_computation.4 | async-start | bytes 131072 | tf_op jit(solution)/shard_map/psum | solution.py:58
  366.2 243.8 %all-reduce.9.cloned.1.call-start = ((), (), s32[]{:S(2)}) async-start(), calls=%async_computation.5 | async-start | bytes 131072 | tf_op jit(solution)/shard_map/psum | solution.py:62
Sparse Core Ops, SparseCore 0:
  9.6 29.8 all-gather.1
  160.4 50.7 reduce-scatter.1
  218.3 119.2 all-reduce.4
  366.3 118.3 all-reduce.6
  491.6 118.3 all-reduce.8
where the time goes:
time: 644 us
  waiting for transfers between devices  446 us (69%)
  other arithmetic  128 us (20%)
  matrix products  39 us (6%)
  local copies, waits for them, and re-layouts  15.6 us (2%)
  between operations  13.9 us (2%)
    psum x1, waiting for transfers between devices, on_device(): lax.psum(jnp.dot(first_part.T, first_part, precision=high), ('row', 'col'))  124 us
    psum x1, waiting for transfers between devices, on_device(): lax.psum(jnp.dot(remainder.T, remainder, precision=high), ('row', 'col'))  122 us
    psum x1, waiting for transfers between devices, on_device(): lax.psum(jnp.dot(basis_one.T, second_part, precision=high), ('row', 'col'))  118 us
    scatter-add x4, other arithmetic, advance(): return summed.at[row_ids].add(product)  77.1 us
    reduce_scatter x1, waiting for transfers between devices, on_device(): lax.psum_scatter(partial_value, 'col', scatter_dimension=0, tiled=True)  50.9 us
    all_gather x1, waiting for transfers between devices, on_device(): gathered = lax.all_gather(gaussian_sketch, 'row', axis=0, tiled=True)  30.8 us
    dot_general x4, matrix products, advance(): jnp.einsum('gab,gbs->gas', values, picked, preferred_element_type=jnp.flo...  29.5 us
    another operation x6, other arithmetic, upper_parts(): lower_factor = jnp.linalg.cholesky(gram)  24.8 us
  transfers between devices with their start and end apart: 5, of which 5 were waited for; matrix products, arithmetic and copies ran while one was open for 0% of the time, Pallas kernels for 0%

commit v1 on v0

--- a/solution.py
+++ b/solution.py
@@ -55,7 +55,11 @@
     upper_one, inverse_one = upper_parts(gram_one)
     basis_one = jnp.dot(first_part, inverse_one, precision=high)
     coupling = (
-        lax.psum(jnp.dot(basis_one.T, second_part, precision=high), ("row", "col")) / order_total
+        jnp.sum(
+            lax.all_gather(jnp.dot(basis_one.T, second_part, precision=high), ("row", "col")),
+            axis=0,
+        )
+        / order_total
     )
     remainder = second_part - jnp.dot(basis_one, coupling, precision=high)
     gram_two = (

time: 644 us -> 581 us (0.902)
  waiting for transfers between devices: 446 us -> 383 us
    psum x1 -> x0, waiting for transfers between devices: 118 us -> none  [on_device(): lax.psum(jnp.dot(basis_one.T, second_part, precision=high), ('row', 'col'))]
    all_gather x0 -> x1, waiting for transfers between devices: none -> 55.8 us  [on_device(): lax.all_gather(jnp.dot(basis_one.T, second_part, precision=high), ('row',...]
where the time goes in v1:
time: 581 us; the launch traced here: 580 us
  waiting for transfers between devices  383 us (66%)
  other arithmetic  129 us (22%)
  matrix products  37.9 us (7%)
  local copies, waits for them, and re-layouts  15.7 us (3%)
  between operations  13.9 us (2%)
    psum x1, waiting for transfers between devices, on_device(): lax.psum(jnp.dot(first_part.T, first_part, precision=high), ('row', 'col'))  124 us
    psum x1, waiting for transfers between devices, on_device(): lax.psum(jnp.dot(remainder.T, remainder, precision=high), ('row', 'col'))  121 us
    scatter-add x4, other arithmetic, advance(): return summed.at[row_ids].add(product)  77.1 us
    all_gather x1, waiting for transfers between devices, on_device(): lax.all_gather(jnp.dot(basis_one.T, second_part, precision=high), ('row',...  55.8 us
    reduce_scatter x1, waiting for transfers between devices, on_device(): lax.psum_scatter(partial_value, 'col', scatter_dimension=0, tiled=True)  50.9 us
    all_gather x1, waiting for transfers between devices, on_device(): gathered = lax.all_gather(gaussian_sketch, 'row', axis=0, tiled=True)  30.8 us
    dot_general x4, matrix products, advance(): jnp.einsum('gab,gbs->gas', values, picked, preferred_element_type=jnp.flo...  29.5 us
    another operation x6, other arithmetic, upper_parts(): lower_factor = jnp.linalg.cholesky(gram)  24.8 us
  transfers between devices with their start and end apart: 5, of which 5 were waited for; matrix products, arithmetic and copies ran while one was open for 0% of the time, Pallas kernels for 0%

profile of v1, /device:TPU:1, one launch (start us, length us, event | category | flops | bytes accessed | tf_op | source)
XLA Modules:
  0.0 580.4 jit_solution(9916369695502082556)
XLA Ops:
  7.2 0.7 all-gather.4.cloned.1.call-update
  8.0 0.7 broadcast_subtract_fusion
  8.7 30.8 %all-gather.4.cloned.1.call-done = bf16[2048,256]{1,0:T(8,128)(2,1)} async-done(((bf16[512,256]{1,0:T(8,128)(2,1)}), bf16[2048,256]{1,0:T(8,128)(2,1)}) %all-gather.4.cloned.1.call-update) | async-done | bytes 1048592 | tf_op jit(solution)/shard_map/all_gather | solution.py:45
  39.5 2.5 broadcast_in_dim.36
  41.9 118.3 %while.13 = (s32[]{:T(128)}, f32[32,128,256]{2,1,0:T(8,128)}, s32[256]{0:T(256)S(1)}, bf16[256,128,128]{2,1,0:T(8,128)(2,1)}, s32[256]{0:T(256)S(1)}, /*index=5*...) while((s32[]{:T(128)}, f32[32,128,256]{2,1,0:T(8,128)}, s32[256]{0:T(256)S(1)}, ...), condition=%wide.region_2.3_spmd, body=%wide.region_0.2_spmd.sunk | while | flops 541066816 | bytes 48240672 | solution.py:31
  42.0 2.8 gather_fusion
  44.8 7.4 %fusion.38 = f32[64,128,256]{2,1,0:T(8,128)} fusion(bf16[64,128,256]{2,1,0:T(8,128)(2,1)} %gather_fusion, pred[64]{0:T(512)(128)(4,1)S(1)} %get-tuple-element.178, bf16[256,128,128]{2,1,0:T(8,128)(2,1)} %get-tuple-element.202, s32[]{:T(128)S(6)} %select_n.59), kind=kOutput, calls=%fused_computation.2.clone.1 | convolution fusion | flops 538968064 | bytes 14680132 | tf_op jit(solution)/shard_map/while/body/eval_jaxpr/gab,gbs->gas/dot_general | solution.py:27
  52.3 19.2 %scatter_fusion = f32[32,128,256]{2,1,0:T(8,128)} fusion(f32[32,128,256]{2,1,0:T(8,128)} %get-tuple-element.190, s32[64]{0:T(128)S(1)} %compare_select_fusion.4, f32[64,128,256]{2,1,0:T(8,128)} %fusion.38), kind=kCustom, calls=%fused_computation.1.clone.1 | custom fusion | flops 2097152 | bytes 25166080 | tf_op jit(solution)/shard_map/while/body/eval_jaxpr/scatter-add | solution.py:28
  71.5 2.8 gather_fusion
  74.3 7.4 %fusion.38 = f32[64,128,256]{2,1,0:T(8,128)} fusion(bf16[64,128,256]{2,1,0:T(8,128)(2,1)} %gather_fusion, pred[64]{0:T(512)(128)(4,1)S(1)} %get-tuple-element.178, bf16[256,128,128]{2,1,0:T(8,128)(2,1)} %get-tuple-element.202, s32[]{:T(128)S(6)} %select_n.59), kind=kOutput, calls=%fused_computation.2.clone.1 | convolution fusion | flops 538968064 | bytes 14680132 | tf_op jit(solution)/shard_map/while/body/eval_jaxpr/gab,gbs->gas/dot_general | solution.py:27
  81.7 19.1 %scatter_fusion = f32[32,128,256]{2,1,0:T(8,128)} fusion(f32[32,128,256]{2,1,0:T(8,128)} %get-tuple-element.190, s32[64]{0:T(128)S(1)} %compare_select_fusion.4, f32[64,128,256]{2,1,0:T(8,128)} %fusion.38), kind=kCustom, calls=%fused_computation.1.clone.1 | custom fusion | flops 2097152 | bytes 25166080 | tf_op jit(solution)/shard_map/while/body/eval_jaxpr/scatter-add | solution.py:28
  101.0 2.8 gather_fusion
  103.7 7.4 %fusion.38 = f32[64,128,256]{2,1,0:T(8,128)} fusion(bf16[64,128,256]{2,1,0:T(8,128)(2,1)} %gather_fusion, pred[64]{0:T(512)(128)(4,1)S(1)} %get-tuple-element.178, bf16[256,128,128]{2,1,0:T(8,128)(2,1)} %get-tuple-element.202, s32[]{:T(128)S(6)} %select_n.59), kind=kOutput, calls=%fused_computation.2.clone.1 | convolution fusion | flops 538968064 | bytes 14680132 | tf_op jit(solution)/shard_map/while/body/eval_jaxpr/gab,gbs->gas/dot_general | solution.py:27
  111.2 19.6 %scatter_fusion = f32[32,128,256]{2,1,0:T(8,128)} fusion(f32[32,128,256]{2,1,0:T(8,128)} %get-tuple-element.190, s32[64]{0:T(128)S(1)} %compare_select_fusion.4, f32[64,128,256]{2,1,0:T(8,128)} %fusion.38), kind=kCustom, calls=%fused_computation.1.clone.1 | custom fusion | flops 2097152 | bytes 25166080 | tf_op jit(solution)/shard_map/while/body/eval_jaxpr/scatter-add | solution.py:28
  130.9 2.8 gather_fusion
  133.6 7.4 %fusion.38 = f32[64,128,256]{2,1,0:T(8,128)} fusion(bf16[64,128,256]{2,1,0:T(8,128)(2,1)} %gather_fusion, pred[64]{0:T(512)(128)(4,1)S(1)} %get-tuple-element.178, bf16[256,128,128]{2,1,0:T(8,128)(2,1)} %get-tuple-element.202, s32[]{:T(128)S(6)} %select_n.59), kind=kOutput, calls=%fused_computation.2.clone.1 | convolution fusion | flops 538968064 | bytes 14680132 | tf_op jit(solution)/shard_map/while/body/eval_jaxpr/gab,gbs->gas/dot_general | solution.py:27
  141.1 19.2 %scatter_fusion = f32[32,128,256]{2,1,0:T(8,128)} fusion(f32[32,128,256]{2,1,0:T(8,128)} %get-tuple-element.190, s32[64]{0:T(128)S(1)} %compare_select_fusion.4, f32[64,128,256]{2,1,0:T(8,128)} %fusion.38), kind=kCustom, calls=%fused_computation.1.clone.1 | custom fusion | flops 2097152 | bytes 25166080 | tf_op jit(solution)/shard_map/while/body/eval_jaxpr/scatter-add | solution.py:28
  160.3 50.9 %reduce-scatter.2.cloned.1.call-done = f32[512,256]{1,0:T(8,128)} async-done(((f32[4096,256]{1,0:T(8,128)}), f32[512,256]{1,0:T(8,128)}) %reduce-scatter.2.cloned.1.call-update) | async-done | bytes 524304 | tf_op jit(solution)/shard_map/reduce_scatter | solution.py:48
  211.2 2.3 fusion.11
  213.6 124.0 %all-reduce.4.cloned.1.call-done = f32[128,128]{0,1:T(8,128)} async-done(((f32[128,128]{0,1:T(8,128)}), f32[128,128]{0,1:T(8,128)}) %all-reduce.4.cloned.1.call-update) | async-done | bytes 65552 | tf_op jit(solution)/shard_map/psum | solution.py:53
  337.6 0.8 broadcast_multiply_fusion.2
  338.5 0.1 copy.13
  338.6 0.9 fusion.20
  339.4 11.7 %cholesky.44 = f32[128,128]{1,0:T(8,128)S(1)} custom-call(f32[128,128]{1,0:T(8,128)S(1)} %fusion.20), custom_call_target="Cholesky" | custom-call | tf_op jit(solution)/shard_map/jit(cholesky)/cholesky | solution.py:11
  351.2 0.6 compare_reduce_fusion.1
  351.8 0.7 fusion.22
  352.5 9.8 %custom-call.6 = f32[1,128,128]{1,2,0:T(8,128)S(1)} custom-call(f32[1,128,128]{2,1,0:T(8,128)S(1)} %get-tuple-element.133), custom_call_target="InvertDiagBlocksLowerTriangular" | custom-call | tf_op jit(solution)/shard_map/triangular_solve/custom-call.0 | solution.py:13
  362.3 0.3 fusion.15
  362.6 1.3 fusion.9
  364.0 2.0 fusion.7
  366.0 0.2 all-reduce.6.cloned.1.call-start
  366.2 55.8 %all-gather.6.cloned.1.call-done = f32[4096,128]{1,0:T(8,128)} async-done(((f32[128,128]{1,0:T(8,128)}), f32[4096,128]{1,0:T(8,128)}) %all-gather.6.cloned.1.call-update) | async-done | bytes 2097168 | tf_op jit(solution)/shard_map/all_gather | solution.py:59
  421.9 1.7 reduce_sum.9
  423.7 0.1 copy.14
  423.8 0.6 convolution_subtract_fusion
  424.4 1.2 fusion.24
  425.6 121.0 %all-reduce.6.cloned.1.call-done = f32[128,128]{0,1:T(8,128)} async-done(((f32[128,128]{0,1:T(8,128)}), f32[128,128]{0,1:T(8,128)}) %all-reduce.6.cloned.1.call-update) | async-done | bytes 65552 | tf_op jit(solution)/shard_map/psum | solution.py:66
  546.7 0.8 broadcast_multiply_fusion
  547.5 0.1 copy.16
  547.6 0.9 fusion.18
  548.5 11.7 %cholesky.55 = f32[128,128]{1,0:T(8,128)S(1)} custom-call(f32[128,128]{1,0:T(8,128)S(1)} %fusion.18), custom_call_target="Cholesky" | custom-call | tf_op jit(solution)/shard_map/jit(cholesky)/cholesky | solution.py:11
  560.2 0.6 compare_reduce_fusion
  560.8 0.7 fusion.23
  561.5 0.8 copy.18
  562.4 9.8 %custom-call.7 = f32[1,128,128]{1,2,0:T(8,128)S(1)} custom-call(f32[1,128,128]{2,1,0:T(8,128)S(1)} %get-tuple-element.135), custom_call_target="InvertDiagBlocksLowerTriangular" | custom-call | tf_op jit(solution)/shard_map/triangular_solve/custom-call.0 | solution.py:13
  572.2 0.3 fusion.13
  572.5 0.4 fusion.25
  572.9 1.0 copy.17
  (29 shorter events, 1.0 us)
Async XLA Ops:
  7.2 32.3 %all-gather.4.cloned.1.call-start = ((), (), s32[]{:S(2)}) async-start(), calls=%async_computation.1 | async-start | bytes 1310720 | tf_op jit(solution)/shard_map/all_gather | solution.py:45
  7.9 203.3 %reduce-scatter.2.cloned.1.call-start = ((), (), s32[]{:S(2)}) async-start(), calls=%async_computation.2 | async-start | bytes 4718592 | tf_op jit(solution)/shard_map/reduce_scatter | solution.py:48
  39.5 2.5 copy-start
  160.3 177.4 %all-reduce.4.cloned.1.call-start = ((), (), s32[]{:S(2)}) async-start(), calls=%async_computation.3 | async-start | bytes 131072 | tf_op jit(solution)/shard_map/psum | solution.py:53
  211.2 212.5 %copy-start.1 = (f32[512,256]{1,0:T(8,128)S(1)}, f32[512,256]{1,0:T(8,128)}, u32[]{:S(2)}) copy-start(f32[512,256]{1,0:T(8,128)} %reduce-scatter.2.cloned.1.call-done) | copy-start | bytes 1572868
  213.6 208.4 %all-gather.6.cloned.1.call-start = ((), (), s32[]{:S(2)}) async-start(), calls=%async_computation.5 | async-start | bytes 2162688 | tf_op jit(solution)/shard_map/all_gather | solution.py:59
  366.0 180.7 %all-reduce.6.cloned.1.call-start = ((), (), s32[]{:S(2)}) async-start(), calls=%async_computation.4 | async-start | bytes 131072 | tf_op jit(solution)/shard_map/psum | solution.py:66
Sparse Core Ops, SparseCore 0:
  9.6 29.8 all-gather.3
  160.4 50.7 reduce-scatter.1
  218.3 119.2 all-reduce.3
  366.1 55.8 all-gather.5
  428.9 117.7 all-reduce.5
